TPU v7x, 32 devices: a whole 2x2x4 slice. The times are simulated.
32 devices in a mesh: dp: 8 (over y, x, core), mp: 4 (over z).
Axes of the slice: x: 2, y: 2, z: 4, core: 2. Of those that a mesh axis runs over, the one named last changes fastest.
Arguments:
- hidden: bfloat16 [24576, 768], P('dp'), may hold values from -6 to 6
- timesteps: int32 [144], P('dp'), may hold values from 0 to 999
- cotangent: bfloat16 [24576, 768], P('dp'), may hold values from -6 to 6
- time_table: bfloat16 [1000, 768], replicated, may hold values from -3 to 3
- first_gain: float32 [768], replicated, may hold values from 0.25 to 1.75
- first_shift: float32 [768], replicated, may hold values from -1.5 to 1.5
- qkv_weight: bfloat16 [3, 768, 768], P(None, None, 'mp'), may hold values from -0.21875 to 0.21875
- out_weight: bfloat16 [768, 768], P('mp'), may hold values from -0.875 to 0.875
- out_bias: float32 [768], replicated, may hold values from -1.5 to 1.5
- second_gain: float32 [768], replicated, may hold values from 0.25 to 1.75
- second_shift: float32 [768], replicated, may hold values from -1.5 to 1.5
- up_weight: bfloat16 [768, 3072], P(None, 'mp'), may hold values from -0.21875 to 0.21875
- up_bias: float32 [3072], P('mp'), may hold values from -2.5 to 2.5
- down_weight: bfloat16 [3072, 768], P('mp'), may hold values from -0.15625 to 0.15625
- down_bias: float32 [768], replicated, may hold values from -1.5 to 1.5
Outputs:
- output: bfloat16 [24576, 768], P('dp')
- grad_hidden: bfloat16 [24576, 768], P('dp')
- grad_table: float32 [1000, 768], P(None, 'mp')
- grad_first_gain: float32 [768], replicated
- grad_first_shift: float32 [768], replicated
- grad_qkv_weight: float32 [3, 768, 768], P(None, 'dp', 'mp')
- grad_out_weight: float32 [768, 768], P('mp', 'dp')
- grad_out_bias: float32 [768], replicated
- grad_second_gain: float32 [768], replicated
- grad_second_shift: float32 [768], replicated
- grad_up_weight: float32 [768, 3072], P('dp', 'mp')
- grad_up_bias: float32 [3072], P('mp')
- grad_down_weight: float32 [3072, 768], P('mp', 'dp')
- grad_down_bias: float32 [768], replicated
All inputs are finite; a program needn't handle non-finite values.
Results may differ from a plain program's by a relative error of at most 0.02.
Values may be sent and summed in bfloat16 or wider, within the bound.
A program may use at most 192 MiB of HBM per device.

v0:
```python
from functools import partial
import jax
import jax.numpy as jnp
from jax import lax
from jax.sharding import PartitionSpec as P

HD = 64
LEN_A = 128
LEN_B = 256
BLOCK = 512


def layer_norm(rows_in, gain_vec, shift_vec):
    centre = jnp.mean(rows_in, axis=-1, keepdims=True)
    offset = rows_in - centre
    spread = jnp.mean(offset * offset, axis=-1, keepdims=True)
    return offset * lax.rsqrt(spread + 1e-05) * gain_vec + shift_vec


def block_scores(queries, key_rows, seg_len):
    scores = jnp.einsum(
        "qhd,khd->hqk", queries, key_rows, preferred_element_type=jnp.float32
    ) * HD ** (-0.5)
    segment = lax.broadcasted_iota(jnp.int32, (BLOCK,), 0) // seg_len
    same_row = segment[:, None] == segment[None, :]
    return jnp.where(same_row[None], scores, -1000000000.0)


def attend_block(queries, key_rows, value_rows, seg_len):
    scores = block_scores(queries, key_rows, seg_len)
    log_total = jax.nn.logsumexp(scores, axis=-1)
    attn_probs = jnp.exp(scores - log_total[..., None]).astype(jnp.bfloat16)
    context = jnp.einsum("hqk,khd->qhd", attn_probs, value_rows, preferred_element_type=jnp.float32)
    return (context, log_total)


def attend_pair(pieces):
    queries, key_rows, value_rows = pieces
    lead_out, lead_log = attend_block(queries[0], key_rows[0], value_rows[0], LEN_A)
    tail_out, tail_log = attend_block(queries[1], key_rows[1], value_rows[1], LEN_B)
    return (jnp.stack([lead_out, tail_out]), jnp.stack([lead_log, tail_log]))


def attend_back_block(queries, key_rows, value_rows, grad_out, log_total, seg_len):
    scores = block_scores(queries, key_rows, seg_len)
    attn_probs = jnp.exp(scores - log_total[..., None])
    grad_probs = jnp.einsum(
        "qhd,khd->hqk", grad_out, value_rows, preferred_element_type=jnp.float32
    )
    grad_values = jnp.einsum(
        "hqk,qhd->khd",
        attn_probs.astype(jnp.bfloat16),
        grad_out,
        preferred_element_type=jnp.float32,
    )
    inner_sum = jnp.sum(attn_probs * grad_probs, axis=-1, keepdims=True)
    grad_scores = (attn_probs * (grad_probs - inner_sum)).astype(jnp.bfloat16)
    scale = HD ** (-0.5)
    grad_queries = (
        jnp.einsum("hqk,khd->qhd", grad_scores, key_rows, preferred_element_type=jnp.float32)
        * scale
    )
    grad_keys = (
        jnp.einsum("hqk,qhd->khd", grad_scores, queries, preferred_element_type=jnp.float32) * scale
    )
    return (grad_queries, grad_keys, grad_values)


def attend_back_pair(pieces):
    queries, key_rows, value_rows, grad_out, log_total = pieces
    lead = attend_back_block(
        queries[0], key_rows[0], value_rows[0], grad_out[0], log_total[0], LEN_A
    )
    tail = attend_back_block(
        queries[1], key_rows[1], value_rows[1], grad_out[1], log_total[1], LEN_B
    )
    return tuple((jnp.stack([lead[index], tail[index]]) for index in range(3)))


def local(
    hidden,
    timesteps,
    cotangent,
    time_table,
    first_gain,
    first_shift,
    qkv_weight,
    out_weight,
    out_bias,
    second_gain,
    second_shift,
    up_weight,
    up_bias,
    down_weight,
    down_bias,
):
    count = hidden.shape[0]
    width = hidden.shape[1]
    local_width = qkv_weight.shape[2]
    local_heads = local_width // HD
    pairs_dev = count // (2 * BLOCK)
    row_count = timesteps.shape[0]
    members = lax.axis_size("mp")
    row_emb = (
        jnp.take(time_table, timesteps, axis=0).astype(jnp.float32).reshape(pairs_dev, 6, width)
    )
    lead_emb = jnp.broadcast_to(row_emb[:, :4, None, :], (pairs_dev, 4, LEN_A, width)).reshape(
        pairs_dev, BLOCK, width
    )
    tail_emb = jnp.broadcast_to(row_emb[:, 4:, None, :], (pairs_dev, 2, LEN_B, width)).reshape(
        pairs_dev, BLOCK, width
    )
    stream_in = jnp.concatenate([lead_emb, tail_emb], axis=1).reshape(count, width) + hidden.astype(
        jnp.float32
    )

    def front(stream_rows):
        normed = layer_norm(stream_rows, first_gain, first_shift).astype(jnp.bfloat16)
        proj = jnp.einsum(
            "td,cde->cte", normed, qkv_weight, preferred_element_type=jnp.float32
        ).astype(jnp.bfloat16)
        shaped = proj.reshape(3, pairs_dev, 2, BLOCK, local_heads, HD)
        context, log_total = lax.map(attend_pair, (shaped[0], shaped[1], shaped[2]))
        return (normed, shaped, context.reshape(count, local_width).astype(jnp.bfloat16), log_total)

    def mlp_front(normed_rows):
        pre_act = jnp.dot(normed_rows, up_weight, preferred_element_type=jnp.float32) + up_bias
        return (pre_act, jax.nn.gelu(pre_act, approximate=True).astype(jnp.bfloat16))

    normed, shaped, context, log_total = front(stream_in)
    attn_part = jnp.dot(context, out_weight, preferred_element_type=jnp.float32)
    attn_total = lax.psum(attn_part.astype(jnp.bfloat16), "mp").astype(jnp.float32)
    middle = stream_in + attn_total + out_bias
    normed_two = layer_norm(middle, second_gain, second_shift).astype(jnp.bfloat16)
    pre_act, activated = mlp_front(normed_two)
    mlp_part = jnp.dot(activated, down_weight, preferred_element_type=jnp.float32)
    result = middle + lax.psum(mlp_part.astype(jnp.bfloat16), "mp").astype(jnp.float32) + down_bias
    grad_top = cotangent.astype(jnp.float32)
    pre_act, activated = mlp_front(lax.optimization_barrier(normed_two))
    grad_down = jnp.einsum("tf,td->fd", activated, cotangent, preferred_element_type=jnp.float32)
    grad_down_bias = jnp.sum(grad_top, axis=0)
    grad_act = jnp.einsum("td,fd->tf", cotangent, down_weight, preferred_element_type=jnp.float32)
    slope_pull = jax.vjp(partial(jax.nn.gelu, approximate=True), pre_act)[1]
    grad_pre = slope_pull(grad_act)[0].astype(jnp.bfloat16)
    grad_up = jnp.einsum("td,tf->df", normed_two, grad_pre, preferred_element_type=jnp.float32)
    grad_up_bias = jnp.sum(grad_pre, axis=0, dtype=jnp.float32)
    norm_part = jnp.einsum("tf,df->td", grad_pre, up_weight, preferred_element_type=jnp.float32)
    norm_grad = lax.psum(norm_part.astype(jnp.bfloat16), "mp").astype(jnp.float32)
    second_pull = jax.vjp(layer_norm, middle, second_gain, second_shift)[1]
    grad_mid, grad_gain_two, grad_shift_two = second_pull(norm_grad)
    grad_mid = grad_mid + grad_top
    grad_mid_low = grad_mid.astype(jnp.bfloat16)
    grad_out_bias = jnp.sum(grad_mid, axis=0)
    normed, shaped, context, log_total = front(lax.optimization_barrier(stream_in))
    grad_out_w = jnp.einsum("te,td->ed", context, grad_mid_low, preferred_element_type=jnp.float32)
    grad_context = jnp.einsum(
        "td,ed->te", grad_mid_low, out_weight, preferred_element_type=jnp.float32
    ).astype(jnp.bfloat16)
    grad_context = grad_context.reshape(pairs_dev, 2, BLOCK, local_heads, HD)
    grad_query, grad_key, grad_value = lax.map(
        attend_back_pair, (shaped[0], shaped[1], shaped[2], grad_context, log_total)
    )
    grad_proj = (
        jnp.stack([grad_query, grad_key, grad_value])
        .reshape(3, count, local_width)
        .astype(jnp.bfloat16)
    )
    grad_qkv = jnp.einsum("td,cte->cde", normed, grad_proj, preferred_element_type=jnp.float32)
    first_part = jnp.einsum(
        "cte,cde->td", grad_proj, qkv_weight, preferred_element_type=jnp.float32
    )
    first_grad = lax.psum(first_part.astype(jnp.bfloat16), "mp").astype(jnp.float32)
    first_pull = jax.vjp(layer_norm, stream_in, first_gain, first_shift)[1]
    grad_in, grad_gain_one, grad_shift_one = first_pull(first_grad)
    grad_in = grad_in + grad_mid
    output = result.astype(jnp.bfloat16)
    columns = width // members
    own_cols = lax.dynamic_slice_in_dim(
        grad_in, lax.axis_index("mp") * columns, columns, 1
    ).reshape(pairs_dev, 2 * BLOCK, columns)
    lead_rows = jnp.sum(own_cols[:, :BLOCK].reshape(pairs_dev, 4, LEN_A, columns), axis=2)
    tail_rows = jnp.sum(own_cols[:, BLOCK:].reshape(pairs_dev, 2, LEN_B, columns), axis=2)
    row_grad = jnp.concatenate([lead_rows, tail_rows], axis=1).reshape(row_count, columns)
    chosen = (
        timesteps[:, None] == lax.broadcasted_iota(jnp.int32, (1, time_table.shape[0]), 1)
    ).astype(jnp.float32)
    table_grad = jnp.dot(
        chosen.T, row_grad, precision=lax.Precision.HIGHEST, preferred_element_type=jnp.float32
    )
    grad_qkv, grad_out_w, grad_up, grad_down = (
        lax.psum_scatter(grad_qkv, "dp", scatter_dimension=1, tiled=True),
        lax.psum_scatter(grad_out_w, "dp", scatter_dimension=1, tiled=True),
        lax.psum_scatter(grad_up, "dp", scatter_dimension=0, tiled=True),
        lax.psum_scatter(grad_down, "dp", scatter_dimension=1, tiled=True),
    )
    (
        table_grad,
        grad_gain_one,
        grad_shift_one,
        grad_out_bias,
        grad_gain_two,
        grad_shift_two,
        grad_up_bias,
        grad_down_bias,
    ) = lax.psum(
        (
            table_grad,
            grad_gain_one,
            grad_shift_one,
            grad_out_bias,
            grad_gain_two,
            grad_shift_two,
            grad_up_bias,
            grad_down_bias,
        ),
        "dp",
    )
    return (
        output,
        grad_in.astype(jnp.bfloat16),
        table_grad,
        grad_gain_one,
        grad_shift_one,
        grad_qkv,
        grad_out_w,
        grad_out_bias,
        grad_gain_two,
        grad_shift_two,
        grad_up,
        grad_up_bias,
        grad_down,
        grad_down_bias,
    )


def solution(mesh):
    return jax.shard_map(
        local,
        mesh=mesh,
        in_specs=(
            P("dp", None),
            P("dp"),
            P("dp", None),
            P(),
            P(),
            P(),
            P(None, None, "mp"),
            P("mp", None),
            P(),
            P(),
            P(),
            P(None, "mp"),
            P("mp"),
            P("mp", None),
            P(),
        ),
        out_specs=(
            P("dp", None),
            P("dp", None),
            P(None, "mp"),
            P(),
            P(),
            P(None, "dp", "mp"),
            P("mp", "dp"),
            P(),
            P(),
            P(),
            P("dp", "mp"),
            P("mp"),
            P("mp", "dp"),
            P(),
        ),
        check_vma=False,
    )
```

profile of v0, /device:TPU:0, one launch (start us, length us, event | category | flops | bytes accessed | tf_op | source)
XLA Modules:
  0.0 1124.5 jit_solution(4650453596753585933)
XLA Ops:
  9.9 2.5 broadcast_in_dim.229
  12.4 6.6 pad_maximum_fusion
  19.0 9.7 fusion.139
  28.8 4.9 multiply_reduce_fusion.4
  35.1 3.5 fusion.104
  40.8 3.5 squeeze.178
  44.3 4.0 squeeze.177
  51.1 31.3 %while.45 = (s32[]{:T(128)}, bf16[3,2,512,3,64]{2,4,3,1,0:T(8,128)(2,1)}, bf16[3,2,512,3,64]{2,1,0,4,3:T(2,128)(2,1)}, bf16[3,2,512,3,64]{2,1,0,4,3:T(2,128)(2,1...) while((s32[]{:T(128)}, bf16[3,2,512,3,64]{2,4,3,1,0:T(8,128)(2,1)}, ...), condition=%wide.region_7.8_spmd, body=%wide.region_2.7_spmd.sunk | while | flops 421284864 | bytes 25809020 | solution.py:123
  53.4 2.4 constant_dynamic-slice_fusion.12
  63.8 2.4 constant_dynamic-slice_fusion.12
  74.2 2.4 constant_dynamic-slice_fusion.12
  82.4 2.5 copy.92
  86.3 3.6 convolution_convert_fusion.2
  90.1 4.2 reduce_sum.301
  94.2 4.8 multiply_reduce_fusion.2
  99.1 5.1 add_convert_fusion
  104.2 2.9 fusion.142
  108.9 4.0 squeeze.181
  112.9 2.5 copy.93
  121.9 143.0 %all-reduce.7.cloned.1.call-done = bf16[3072,768]{1,0:T(8,128)(2,1)} async-done(((bf16[3072,768]{1,0:T(8,128)(2,1)}), bf16[3072,768]{1,0:T(8,128)(2,1)}) %all-reduce.7.cloned.1.call-update) | async-done | bytes 4718608 | tf_op jit(solution)/shard_map/psum | solution.py:132
  264.8 10.0 fusion.138
  274.9 4.9 multiply_reduce_fusion.3
  283.0 6.3 fusion.143
  289.4 12.0 %convert_reduce_fusion.3 = (f32[768]{0:T(1024)}, bf16[3072,768]{1,0:T(8,128)(2,1)S(1)}) fusion(f32[3072,768]{1,0:T(8,128)} %fusion.143, f32[768]{0:T(1024)S(1)} %copy-done.37, bf16[3072,768]{1,0:T(8,128)(2,1)S(1)} %bitcast.369, bf16[768,768]{1,0:T(8,128)(2,1)S(1)} %copy-done.33), kind=kOutput, calls=%fused_computation.213 | convolution fusion | flops 3678141696 | bytes 20060160 | tf_op jit(solution)/shard_map/td,fd->tf/dot_general | solution.py:142
  301.4 2.2 copy-done.39
  303.6 5.5 convolution_convert_fusion
  310.3 24.6 %while.46 = (s32[]{:T(128)}, bf16[3,2,512,3,64]{2,4,3,1,0:T(8,128)(2,1)}, f32[3,2,3,512]{3,2,1,0:T(4,128)S(1)}, bf16[3,2,512,3,64]{2,4,3,1,0:T(8,128)(2,1)}, bf1...) while((s32[]{:T(128)}, ...), condition=%wide.region_22.23_spmd, body=%wide.region_17.22_spmd.sunk | while | flops 421300224 | bytes 23522436 | solution.py:123
  315.7 1.9 fusion.210
  320.5 1.9 fusion.213
  323.9 1.9 fusion.210
  332.1 1.9 fusion.210
  334.9 3.5 copy.103
  338.4 3.9 convert_element_type.176
  342.3 137.8 %all-reduce.9.cloned.1.call-done = bf16[3072,768]{1,0:T(8,128)(2,1)} async-done(((bf16[3072,768]{1,0:T(8,128)(2,1)}), bf16[3072,768]{1,0:T(8,128)(2,1)}) %all-reduce.9.cloned.1.call-update) | async-done | bytes 4718608 | tf_op jit(solution)/shard_map/psum | solution.py:148
  480.2 8.4 convert_reduce_fusion.1
  488.6 8.3 fusion.102
  497.0 5.4 fusion.136
  502.4 3.3 convolution_convert_fusion.3
  506.5 2.9 fusion.118
  509.5 4.4 reshape.677
  517.3 43.6 %while.47 = (s32[]{:T(128)}, bf16[3,2,512,3,64]{2,4,3,1,0:T(8,128)(2,1)}, bf16[3,2,512,3,64]{2,4,3,1,0:T(8,128)(2,1)}, bf16[3,2,512,3,64]{2,4,3,1,0:T(8,128)(2,1...) while((s32[]{:T(128)}, ...), condition=%wide.region_26.27_spmd, body=%wide.region_23.26_spmd.sunk | while | flops 1024463872 | bytes 55389380 | solution.py:160
  561.0 3.5 copy.102
  564.5 3.6 stack.128
  568.0 3.5 copy.100
  571.6 3.9 stack.126
  575.5 2.3 copy.101
  577.8 3.3 stack.127
  584.4 5.2 fusion.115
  589.6 2.7 copy.115
  592.3 4.8 reshape.697
  597.3 12.6 %convolution_convert_fusion.1 = bf16[3072,768]{1,0:T(8,128)(2,1)} fusion(bf16[768,768]{1,0:T(8,128)(2,1)S(1)} %copy-done.34, bf16[3072,768]{1,0:T(8,128)(2,1)} %copy-done.7, bf16[768,768]{1,0:T(8,128)(2,1)S(1)} %copy-done.32, f32[768]{0:T(1024)S(1)} %copy-done.38), kind=kOutput, calls=%fused_computation.224 | convolution fusion | flops 7273709568 | bytes 11799552 | tf_op jit(solution)/shard_map/dot_general | solution.py:136
  609.8 8.2 bitcast_convert_fusion
  618.1 9.1 fusion.144
  627.6 11.5 %fusion.111 = f32[768,768]{0,1:T(8,128)} fusion(bf16[3072,768]{1,0:T(8,128)(2,1)} %param.23, f32[3072,768]{1,0:T(8,128)} %fusion.143, f32[768]{0:T(1024)S(1)} %copy-done.38), kind=kOutput, calls=%fused_computation.233 | convolution fusion | flops 3647471616 | bytes 16518144 | tf_op jit(solution)/shard_map/tf,td->fd/dot_general | solution.py:140
  642.8 321.4 %all-reduce.13.cloned.1.call-done = (bf16[3072,768]{1,0:T(8,128)(2,1)}, bf16[3072,768]{1,0:T(8,128)(2,1)}) async-done(((bf16[3072,768]{1,0:T(8,128)(2,1)}, bf16[3072,768]{1,0:T(8,128)(2,1)}), (bf16[3072,768]{1,0:T(8,128)(2,1)}, bf16[3072,768]{1,0:T(8,128)(2,1)})) %all-reduce.13.cloned.1.call-update) | async-done | bytes 9437200 | tf_op jit(solution)/shard_map/psum | solution.py:137
  964.2 8.4 convert_reduce_fusion
  972.7 10.3 fusion.103
  983.2 6.6 fusion.137
  989.8 3.2 constant_dynamic-slice_fusion.8
  994.8 8.6 add_convert_fusion.1
  1003.5 24.4 %all-reduce = (f32[768]{0:T(1024)}, f32[768]{0:T(1024)}, f32[768]{0:T(1024)}, f32[768]{0:T(1024)}, f32[768]{0:T(1024)}, /*index=5*/f32[768]{0:T(1024)}, f32[768]{0:T(1024)}) all-reduce(f32[768]{0:T(1024)S(1)} %get-tuple-element.458, f32[768]{0:T(1024)S(1)} %get-tuple-element.462, ...), channel_id=1, replica_groups=mesh['dp'=8,'mp'=4] {'dp'}, use_global_device_ids=true, to_apply=%region_34.35 | all-reduce | flops 5376 | bytes 43008 | tf_op jit(solution)/shard_map/psum | solution.py:205
  1027.9 27.8 %reduce-scatter.11.cloned.1.call-done = f32[768,96]{0,1:T(8,128)} async-done(((f32[768,768]{0,1:T(8,128)}), f32[768,96]{0,1:T(8,128)}) %reduce-scatter.11.cloned.1.call-update) | async-done | bytes 294928 | tf_op jit(solution)/shard_map/reduce_scatter | solution.py:194
  1055.7 59.4 %all-reduce.11.cloned.1.call-done = f32[1000,192]{0,1:T(8,128)} async-done(((f32[1000,192]{0,1:T(8,128)}), f32[1000,192]{0,1:T(8,128)}) %all-reduce.11.cloned.1.call-update) | async-done | bytes 768016 | tf_op jit(solution)/shard_map/psum | solution.py:205
  1115.1 2.1 copy.219
  (334 shorter events, 120.3 us)
Async XLA Ops:
  7.2 1.6 copy-start
  7.2 257.6 %all-reduce.7.cloned.1.call-start = ((), (), s32[]{:S(2)}) async-start(), calls=%async_computation.4 | async-start | bytes 9437184 | tf_op jit(solution)/shard_map/psum | solution.py:132
  19.0 14.8 %copy-start.35 = (bf16[3,768,192]{1,2,0:T(8,128)(2,1)S(1)}, bf16[3,768,192]{1,2,0:T(8,128)(2,1)}, u32[]{:S(2)}) copy-start(bf16[3,768,192]{1,2,0:T(8,128)(2,1)} %param.27) | copy-start | bytes 2654212
  28.7 5.0 copy-start.12
  28.7 6.4 copy-start.2
  28.8 6.4 copy-start.19
  28.8 6.4 copy-start.25
  33.7 4.9 copy-start.14
  33.8 4.9 copy-start.16
  82.4 3.9 copy-start.10
  90.0 390.2 %all-reduce.9.cloned.1.call-start = ((), (), s32[]{:S(2)}) async-start(), calls=%async_computation.5 | async-start | bytes 9437184 | tf_op jit(solution)/shard_map/psum | solution.py:148
  99.1 5.1 copy-start.36
  104.2 3.0 copy-start.6
  117.2 147.7 %copy-start.26 = (f32[768]{0:T(1024)S(1)}, f32[768]{0:T(1024)}, u32[]{:S(2)}) copy-start(f32[768]{0:T(1024)} %param.29) | copy-start | bytes 9220
  274.8 6.4 copy-start.3
  274.9 6.4 copy-start.18
  274.9 6.4 copy-start.27
  281.2 1.7 copy-start.31
  281.2 8.1 slice-start.11
  282.9 6.4 copy-start.7
  283.0 6.4 slice-start.12
  283.0 6.4 copy-start.33
  283.0 6.4 copy-start.37
  301.4 2.2 copy-start.39
  309.1 330.2 %reduce-scatter.15.cloned.1.call-start = ((), (), s32[]{:S(2)}) async-start(), calls=%async_computation.10 | async-start | bytes 884736
  480.2 8.4 copy-start.5
  480.2 16.8 %slice-start.3 = ((s8[9437184]{0:T(1024)(128)(4,1)}), s8[4194304]{0:T(1024)(128)(4,1)S(1)}, s32[]{:S(2)}) async-start(s8[9437184]{0:T(1024)(128)(4,1)} %bitcast.355), calls=%async_computation.15 | async-start | bytes 8388608
  480.2 16.8 %slice-start.4 = ((s8[9437184]{0:T(1024)(128)(4,1)}), s8[4194304]{0:T(1024)(128)(4,1)S(1)}, s32[]{:S(2)}) async-start(s8[9437184]{0:T(1024)(128)(4,1)} %bitcast.355), calls=%async_computation.16 | async-start | bytes 8388608
  480.2 16.8 %slice-start.13 = ((s8[4718592]{0:T(1024)(128)(4,1)}), s8[4194304]{0:T(1024)(128)(4,1)S(1)}, s32[]{:S(2)}) async-start(s8[4718592]{0:T(1024)(128)(4,1)} %bitcast.370), calls=%async_computation.25 | async-start | bytes 8388608
  488.6 8.4 slice-start.5
  488.6 8.4 slice-start.14
  502.4 4.0 copy-start.4
  502.4 4.0 copy-start.9
  509.4 131.4 %reduce-scatter.13.cloned.1.call-start = ((), (), s32[]{:S(2)}) async-start(), calls=%async_computation.9 | async-start | bytes 2211840
  564.5 11.0 copy-start.8
  582.6 1.8 copy-start.11
  592.3 4.9 copy-start.32
  592.3 4.9 copy-start.34
  592.3 4.9 copy-start.38
  597.2 367.0 %all-reduce.13.cloned.1.call-start = ((), (), s32[]{:S(2)}) async-start(), calls=%async_computation.11 | async-start | bytes 18874368 | tf_op jit(solution)/shard_map/psum | solution.py:137
  618.1 409.8 %reduce-scatter.9.cloned.1.call-start = ((), (), s32[]{:S(2)}) async-start(), calls=%async_computation.7 | async-start | bytes 2654208 | tf_op jit(solution)/shard_map/reduce_scatter | solution.py:193
  627.3 428.4 %reduce-scatter.11.cloned.1.call-start = ((), (), s32[]{:S(2)}) async-start(), calls=%async_computation.8 | async-start | bytes 2654208 | tf_op jit(solution)/shard_map/reduce_scatter | solution.py:194
  627.6 345.1 %copy-start.15 = (f32[3072]{0:T(1024)S(1)}, f32[3072]{0:T(1024)}, u32[]{:S(2)}) copy-start(f32[3072]{0:T(1024)} %copy-done.14) | copy-start | bytes 36868
  627.6 345.1 %copy-start.17 = (f32[3072]{0:T(1024)S(1)}, f32[3072]{0:T(1024)}, u32[]{:S(2)}) copy-start(f32[3072]{0:T(1024)} %copy-done.16) | copy-start | bytes 36868
  639.2 325.0 %copy-start.13 = (f32[3072]{0:T(1024)S(1)}, f32[3072]{0:T(1024)}, u32[]{:S(2)}) copy-start(f32[3072]{0:T(1024)} %copy-done.12) | copy-start | bytes 36868
  639.2 325.0 %copy-start.20 = (f32[768]{0:T(1024)S(1)}, f32[768]{0:T(1024)}, u32[]{:S(2)}) copy-start(f32[768]{0:T(1024)} %param.25) | copy-start | bytes 9220
  639.2 475.9 %all-reduce.11.cloned.1.call-start = ((), (), s32[]{:S(2)}) async-start(), calls=%async_computation.6 | async-start | bytes 1572864 | tf_op jit(solution)/shard_map/psum | solution.py:205
  964.2 18.9 %slice-start = ((s8[9437184]{0:T(1024)(128)(4,1)}), s8[4194304]{0:T(1024)(128)(4,1)S(1)}, s32[]{:S(2)}) async-start(s8[9437184]{0:T(1024)(128)(4,1)} %bitcast.353), calls=%async_computation.12 | async-start | bytes 8388608
  964.2 18.9 %slice-start.1 = ((s8[9437184]{0:T(1024)(128)(4,1)}), s8[4194304]{0:T(1024)(128)(4,1)S(1)}, s32[]{:S(2)}) async-start(s8[9437184]{0:T(1024)(128)(4,1)} %bitcast.353), calls=%async_computation.13 | async-start | bytes 8388608
  964.2 18.9 %slice-start.6 = ((s8[9437184]{0:T(1024)(128)(4,1)}), s8[4194304]{0:T(1024)(128)(4,1)S(1)}, s32[]{:S(2)}) async-start(s8[9437184]{0:T(1024)(128)(4,1)} %bitcast.357), calls=%async_computation.18 | async-start | bytes 8388608
  964.2 18.9 %slice-start.7 = ((s8[9437184]{0:T(1024)(128)(4,1)}), s8[4194304]{0:T(1024)(128)(4,1)S(1)}, s32[]{:S(2)}) async-start(s8[9437184]{0:T(1024)(128)(4,1)} %bitcast.357), calls=%async_computation.19 | async-start | bytes 8388608
  964.2 18.9 %slice-start.9 = ((s8[4718592]{0:T(1024)(128)(4,1)}), s8[4194304]{0:T(1024)(128)(4,1)S(1)}, s32[]{:S(2)}) async-start(s8[4718592]{0:T(1024)(128)(4,1)} %bitcast.359), calls=%async_computation.21 | async-start | bytes 8388608
  972.7 10.4 slice-start.2
  972.7 10.4 slice-start.8
  972.7 10.4 slice-start.10
  989.8 3.5 copy-start.30
  993.0 1.8 copy-start.28
  994.8 8.7 copy-start.21
  994.8 8.7 copy-start.22
  994.8 8.7 copy-start.23
  994.8 8.7 copy-start.24
  994.8 8.7 copy-start.29
  994.8 122.4 %copy-start.1 = (bf16[1000,768]{1,0:T(8,128)(2,1)S(1)}, bf16[1000,768]{1,0:T(8,128)(2,1)}, u32[]{:S(2)}) copy-start(bf16[1000,768]{1,0:T(8,128)(2,1)} %param.24) | copy-start | bytes 4608004
Sparse Core Ops, SparseCore 0:
  90.1 174.6 all-reduce.6
  309.2 170.9 all-reduce.8
  509.6 33.9 reduce-scatter.14
  597.3 39.1 reduce-scatter.12
  639.5 324.6 all-reduce.12
  968.0 41.3 reduce-scatter.8
  1013.2 42.3 reduce-scatter.10
  1059.4 55.6 all-reduce.10
where the time goes:
time: 1130 us; the launch traced here: 1120 us
  waiting for transfers between devices  690 us (61%)
  matrix products  141 us (12%)
  other arithmetic  139 us (12%)
  local copies, waits for them, and re-layouts  114 us (10%)
  blocking collectives  24.4 us (2%)
  between operations  15.4 us (1%)
    psum x1, waiting for transfers between devices, local(): lax.psum(mlp_part.astype(jnp.bfloat16), 'mp').astype(jnp.float32)  321 us
    psum x1, waiting for transfers between devices, local(): lax.psum(attn_part.astype(jnp.bfloat16), 'mp').astype(jnp.float32)  143 us
    psum x1, waiting for transfers between devices, local(): lax.psum(norm_part.astype(jnp.bfloat16), 'mp').astype(jnp.float32)  138 us
    psum x1, waiting for transfers between devices, local(): lax.psum((table_grad, grad_gain_one, grad_shift_one, grad_out_bias, grad_...  59.4 us
    reduce_sum x4, other arithmetic, layer_norm(): return offset * lax.rsqrt(spread + 1e-05) * gain_vec + shift_vec  35.5 us
    reduce_scatter x1, waiting for transfers between devices, local(): lax.psum_scatter(grad_down, 'dp', scatter_dimension=1, tiled=True)  27.8 us
    psum x1, blocking collectives, local(): lax.psum((table_grad, grad_gain_one, grad_shift_one, grad_out_bias, grad_...  24.4 us
    reduce_sum x3, other arithmetic, layer_norm(): centre = jnp.mean(rows_in, axis=-1, keepdims=True)  23.9 us
  transfers between devices with their start and end apart: 8, of which 5 were waited for; matrix products, arithmetic and copies ran while one was open for 21% of the time, Pallas kernels for 0%

commit v1 on v0

--- a/solution.py
+++ b/solution.py
@@ -129,7 +129,9 @@
 
     normed, shaped, context, log_total = front(stream_in)
     attn_part = jnp.dot(context, out_weight, preferred_element_type=jnp.float32)
-    attn_total = lax.psum(attn_part.astype(jnp.bfloat16), "mp").astype(jnp.float32)
+    attn_total = jnp.sum(lax.all_gather(attn_part.astype(jnp.bfloat16), "mp"), axis=0).astype(
+        jnp.float32
+    )
     middle = stream_in + attn_total + out_bias
     normed_two = layer_norm(middle, second_gain, second_shift).astype(jnp.bfloat16)
     pre_act, activated = mlp_front(normed_two)

time: 1130 us -> 1300 us (1.15)
  waiting for transfers between devices: 690 us -> 839 us
  other arithmetic: 139 us -> 154 us
    all_gather x0 -> x1, waiting for transfers between devices: none -> 292 us  [local(): lax.all_gather(attn_part.astype(jnp.bfloat16), 'mp')]
    psum x1 -> x0, waiting for transfers between devices: 143 us -> none  [local(): lax.psum(attn_part.astype(jnp.bfloat16), 'mp').astype(jnp.float32)]
    reduce_sum x0 -> x1, other arithmetic: none -> 13.6 us  [local(): jnp.sum(lax.all_gather(attn_part.astype(jnp.bfloat16), 'mp'), axis=0)]
  transfers between devices with their start and end apart: 8 -> 8, of which waited for: 5 -> 5; matrix products, arithmetic and copies ran while one was open for 21% -> 18% of each run, Pallas kernels for 0% -> 0%
where the time goes in v1:
time: 1300 us; the launch traced here: 1290 us
  waiting for transfers between devices  839 us (65%)
  other arithmetic  154 us (12%)
  matrix products  141 us (11%)
  local copies, waits for them, and re-layouts  114 us (9%)
  blocking collectives  24.3 us (2%)
  between operations  15.4 us (1%)
    psum x1, waiting for transfers between devices, local(): lax.psum(mlp_part.astype(jnp.bfloat16), 'mp').astype(jnp.float32)  321 us
    all_gather x1, waiting for transfers between devices, local(): lax.all_gather(attn_part.astype(jnp.bfloat16), 'mp')  292 us
    psum x1, waiting for transfers between devices, local(): lax.psum(norm_part.astype(jnp.bfloat16), 'mp').astype(jnp.float32)  138 us
    psum x1, waiting for transfers between devices, local(): lax.psum((table_grad, grad_gain_one, grad_shift_one, grad_out_bias, grad_...  59.4 us
    reduce_sum x4, other arithmetic, layer_norm(): return offset * lax.rsqrt(spread + 1e-05) * gain_vec + shift_vec  35.6 us
    reduce_scatter x1, waiting for transfers between devices, local(): lax.psum_scatter(grad_down, 'dp', scatter_dimension=1, tiled=True)  27.8 us
  transfers between devices with their start and end apart: 8, of which 5 were waited for; matrix products, arithmetic and copies ran while one was open for 18% of the time, Pallas kernels for 0%

profile of v1, /device:TPU:0, one launch (start us, length us, event | category | flops | bytes accessed | tf_op | source)
XLA Modules:
  0.0 1288.6 jit_solution(6825914234867102181)
XLA Ops:
  9.9 2.5 broadcast_in_dim.229
  12.4 6.6 pad_maximum_fusion
  19.0 9.8 fusion.139
  28.8 4.9 multiply_reduce_fusion.4
  35.2 3.5 fusion.104
  40.8 3.5 squeeze.178
  44.4 4.0 squeeze.177
  51.1 31.5 %while.45 = (s32[]{:T(128)}, bf16[3,2,512,3,64]{2,4,3,1,0:T(8,128)(2,1)}, bf16[3,2,512,3,64]{2,1,0,4,3:T(2,128)(2,1)}, bf16[3,2,512,3,64]{2,1,0,4,3:T(2,128)(2,1...) while((s32[]{:T(128)}, bf16[3,2,512,3,64]{2,4,3,1,0:T(8,128)(2,1)}, ...), condition=%wide.region_7.8_spmd, body=%wide.region_2.7_spmd.sunk | while | flops 421284864 | bytes 25809020 | solution.py:123
  53.4 2.5 constant_dynamic-slice_fusion.12
  63.9 2.4 constant_dynamic-slice_fusion.12
  74.3 2.5 constant_dynamic-slice_fusion.12
  82.6 2.5 copy.92
  86.5 3.6 convolution_convert_fusion.2
  90.3 4.2 reduce_sum.314
  94.5 4.8 multiply_reduce_fusion.2
  99.4 6.4 add_convert_fusion
  105.8 2.9 fusion.142
  110.5 4.0 squeeze.181
  114.6 2.5 copy.93
  123.5 292.1 %all-gather.3.cloned.1.call-done = bf16[12288,768]{1,0:T(8,128)(2,1)} async-done(((bf16[3072,768]{1,0:T(8,128)(2,1)}), bf16[12288,768]{1,0:T(8,128)(2,1)}) %all-gather.3.cloned.1.call-update) | async-done | bytes 18874384 | tf_op jit(solution)/shard_map/all_gather | solution.py:132
  415.7 13.6 %reduce_sum.311 = bf16[3072,768]{1,0:T(8,128)(2,1)} reduce(bf16[4,3072,768]{2,1,0:T(8,128)(2,1)} %bitcast.362, bf16[]{:T(256)} %constant.349.clone.1), dimensions={0}, to_apply=%region_8.9 | reduce | flops 7077888 | bytes 23592962 | tf_op jit(solution)/shard_map/reduce_sum | solution.py:132
  429.2 10.0 fusion.138
  439.2 4.9 multiply_reduce_fusion.3
  447.3 6.4 fusion.143
  453.8 11.9 convert_reduce_fusion.3
  465.7 2.2 copy-done.39
  467.9 5.5 convolution_convert_fusion
  474.6 24.6 %while.46 = (s32[]{:T(128)}, bf16[3,2,512,3,64]{2,4,3,1,0:T(8,128)(2,1)}, f32[3,2,3,512]{3,2,1,0:T(4,128)S(1)}, bf16[3,2,512,3,64]{2,4,3,1,0:T(8,128)(2,1)}, bf1...) while((s32[]{:T(128)}, ...), condition=%wide.region_22.23_spmd, body=%wide.region_17.22_spmd.sunk | while | flops 421300224 | bytes 23522436 | solution.py:123
  476.6 1.9 fusion.213
  480.1 1.9 fusion.210
  488.3 1.9 fusion.210
  499.2 3.5 copy.103
  502.7 3.9 convert_element_type.178
  506.6 137.7 %all-reduce.6.cloned.1.call-done = bf16[3072,768]{1,0:T(8,128)(2,1)} async-done(((bf16[3072,768]{1,0:T(8,128)(2,1)}), bf16[3072,768]{1,0:T(8,128)(2,1)}) %all-reduce.6.cloned.1.call-update) | async-done | bytes 4718608 | tf_op jit(solution)/shard_map/psum | solution.py:150
  644.4 8.4 convert_reduce_fusion.1
  652.8 8.3 fusion.102
  661.2 5.4 fusion.136
  666.6 3.3 convolution_convert_fusion.3
  670.7 2.9 fusion.118
  673.7 4.4 reshape.677
  681.5 43.6 %while.47 = (s32[]{:T(128)}, bf16[3,2,512,3,64]{2,4,3,1,0:T(8,128)(2,1)}, bf16[3,2,512,3,64]{2,4,3,1,0:T(8,128)(2,1)}, bf16[3,2,512,3,64]{2,4,3,1,0:T(8,128)(2,1...) while((s32[]{:T(128)}, ...), condition=%wide.region_26.27_spmd, body=%wide.region_23.26_spmd.sunk | while | flops 1024463872 | bytes 55389380 | solution.py:162
  725.1 3.5 copy.102
  728.7 3.6 stack.128
  732.2 3.5 copy.100
  735.8 3.9 stack.126
  739.7 2.3 copy.101
  742.0 3.3 stack.127
  748.6 5.2 fusion.115
  753.8 2.7 copy.115
  756.5 4.8 reshape.698
  761.5 12.6 convolution_convert_fusion.1
  774.0 8.2 bitcast_convert_fusion
  782.3 9.1 fusion.144
  791.8 11.5 fusion.111
  807.0 321.4 %all-reduce.10.cloned.1.call-done = (bf16[3072,768]{1,0:T(8,128)(2,1)}, bf16[3072,768]{1,0:T(8,128)(2,1)}) async-done(((bf16[3072,768]{1,0:T(8,128)(2,1)}, bf16[3072,768]{1,0:T(8,128)(2,1)}), (bf16[3072,768]{1,0:T(8,128)(2,1)}, bf16[3072,768]{1,0:T(8,128)(2,1)})) %all-reduce.10.cloned.1.call-update) | async-done | bytes 9437200 | tf_op jit(solution)/shard_map/psum | solution.py:139
  1128.4 8.7 convert_reduce_fusion
  1137.2 10.2 fusion.103
  1147.4 6.6 fusion.137
  1154.0 3.2 constant_dynamic-slice_fusion.8
  1159.1 8.6 add_convert_fusion.1
  1167.8 24.3 %all-reduce = (f32[768]{0:T(1024)}, f32[768]{0:T(1024)}, f32[768]{0:T(1024)}, f32[768]{0:T(1024)}, f32[768]{0:T(1024)}, /*index=5*/f32[768]{0:T(1024)}, f32[768]{0:T(1024)}) all-reduce(f32[768]{0:T(1024)S(1)} %get-tuple-element.458, f32[768]{0:T(1024)S(1)} %get-tuple-element.462, ...), channel_id=1, replica_groups=mesh['dp'=8,'mp'=4] {'dp'}, use_global_device_ids=true, to_apply=%region_34.35 | all-reduce | flops 5376 | bytes 43008 | tf_op jit(solution)/shard_map/psum | solution.py:207
  1192.1 27.8 %reduce-scatter.11.cloned.1.call-done = f32[768,96]{0,1:T(8,128)} async-done(((f32[768,768]{0,1:T(8,128)}), f32[768,96]{0,1:T(8,128)}) %reduce-scatter.11.cloned.1.call-update) | async-done | bytes 294928 | tf_op jit(solution)/shard_map/reduce_scatter | solution.py:196
  1219.8 59.4 %all-reduce.8.cloned.1.call-done = f32[1000,192]{0,1:T(8,128)} async-done(((f32[1000,192]{0,1:T(8,128)}), f32[1000,192]{0,1:T(8,128)}) %all-reduce.8.cloned.1.call-update) | async-done | bytes 768016 | tf_op jit(solution)/shard_map/psum | solution.py:207
  1279.3 2.1 copy.218
  (335 shorter events, 122.2 us)
Async XLA Ops:
  7.2 1.6 copy-start
  7.2 408.5 %all-gather.3.cloned.1.call-start = ((), (), s32[]{:S(2)}) async-start(), calls=%async_computation.8 | async-start | bytes 23592960 | tf_op jit(solution)/shard_map/all_gather | solution.py:132
  19.0 14.8 %copy-start.35 = (bf16[3,768,192]{1,2,0:T(8,128)(2,1)S(1)}, bf16[3,768,192]{1,2,0:T(8,128)(2,1)}, u32[]{:S(2)}) copy-start(bf16[3,768,192]{1,2,0:T(8,128)(2,1)} %param.27) | copy-start | bytes 2654212
  28.8 5.0 copy-start.12
  28.8 6.4 copy-start.2
  28.8 6.4 copy-start.19
  28.8 6.4 copy-start.25
  33.8 4.9 copy-start.14
  33.8 4.9 copy-start.16
  82.6 3.9 copy-start.10
  90.2 554.2 %all-reduce.6.cloned.1.call-start = ((), (), s32[]{:S(2)}) async-start(), calls=%async_computation.4 | async-start | bytes 9437184 | tf_op jit(solution)/shard_map/psum | solution.py:150
  99.4 6.4 copy-start.36
  105.8 3.0 copy-start.6
  415.7 13.6 %copy-start.26 = (f32[768]{0:T(1024)S(1)}, f32[768]{0:T(1024)}, u32[]{:S(2)}) copy-start(f32[768]{0:T(1024)} %param.29) | copy-start | bytes 9220
  439.2 6.4 copy-start.3
  439.2 6.4 copy-start.18
  439.2 6.4 copy-start.27
  445.6 1.7 copy-start.31
  445.6 8.3 slice-start.11
  447.3 6.5 copy-start.7
  447.3 6.5 slice-start.12
  447.3 6.5 copy-start.33
  447.3 6.5 copy-start.37
  465.7 2.2 copy-start.39
  473.4 330.0 %reduce-scatter.15.cloned.1.call-start = ((), (), s32[]{:S(2)}) async-start(), calls=%async_computation.10 | async-start | bytes 884736
  644.4 8.4 copy-start.5
  644.4 16.8 %slice-start.3 = ((s8[9437184]{0:T(1024)(128)(4,1)}), s8[4194304]{0:T(1024)(128)(4,1)S(1)}, s32[]{:S(2)}) async-start(s8[9437184]{0:T(1024)(128)(4,1)} %bitcast.356), calls=%async_computation.15 | async-start | bytes 8388608
  644.4 16.8 %slice-start.4 = ((s8[9437184]{0:T(1024)(128)(4,1)}), s8[4194304]{0:T(1024)(128)(4,1)S(1)}, s32[]{:S(2)}) async-start(s8[9437184]{0:T(1024)(128)(4,1)} %bitcast.356), calls=%async_computation.16 | async-start | bytes 8388608
  644.4 16.8 %slice-start.13 = ((s8[4718592]{0:T(1024)(128)(4,1)}), s8[4194304]{0:T(1024)(128)(4,1)S(1)}, s32[]{:S(2)}) async-start(s8[4718592]{0:T(1024)(128)(4,1)} %bitcast.372), calls=%async_computation.25 | async-start | bytes 8388608
  652.8 8.4 slice-start.5
  652.8 8.4 slice-start.14
  666.6 4.0 copy-start.4
  666.6 4.0 copy-start.9
  673.6 131.4 %reduce-scatter.13.cloned.1.call-start = ((), (), s32[]{:S(2)}) async-start(), calls=%async_computation.9 | async-start | bytes 2211840
  728.7 11.0 copy-start.8
  746.8 1.8 copy-start.11
  756.5 4.9 copy-start.32
  756.5 4.9 copy-start.34
  756.5 4.9 copy-start.38
  761.4 367.0 %all-reduce.10.cloned.1.call-start = ((), (), s32[]{:S(2)}) async-start(), calls=%async_computation.11 | async-start | bytes 18874368 | tf_op jit(solution)/shard_map/psum | solution.py:139
  782.3 409.8 %reduce-scatter.9.cloned.1.call-start = ((), (), s32[]{:S(2)}) async-start(), calls=%async_computation.6 | async-start | bytes 2654208 | tf_op jit(solution)/shard_map/reduce_scatter | solution.py:195
  791.5 428.4 %reduce-scatter.11.cloned.1.call-start = ((), (), s32[]{:S(2)}) async-start(), calls=%async_computation.7 | async-start | bytes 2654208 | tf_op jit(solution)/shard_map/reduce_scatter | solution.py:196
  791.8 345.3 %copy-start.15 = (f32[3072]{0:T(1024)S(1)}, f32[3072]{0:T(1024)}, u32[]{:S(2)}) copy-start(f32[3072]{0:T(1024)} %copy-done.14) | copy-start | bytes 36868
  791.8 345.3 %copy-start.17 = (f32[3072]{0:T(1024)S(1)}, f32[3072]{0:T(1024)}, u32[]{:S(2)}) copy-start(f32[3072]{0:T(1024)} %copy-done.16) | copy-start | bytes 36868
  803.3 325.0 %copy-start.13 = (f32[3072]{0:T(1024)S(1)}, f32[3072]{0:T(1024)}, u32[]{:S(2)}) copy-start(f32[3072]{0:T(1024)} %copy-done.12) | copy-start | bytes 36868
  803.3 325.0 %copy-start.20 = (f32[768]{0:T(1024)S(1)}, f32[768]{0:T(1024)}, u32[]{:S(2)}) copy-start(f32[768]{0:T(1024)} %param.25) | copy-start | bytes 9220
  803.4 475.9 %all-reduce.8.cloned.1.call-start = ((), (), s32[]{:S(2)}) async-start(), calls=%async_computation.5 | async-start | bytes 1572864 | tf_op jit(solution)/shard_map/psum | solution.py:207
  1128.4 19.0 %slice-start = ((s8[9437184]{0:T(1024)(128)(4,1)}), s8[4194304]{0:T(1024)(128)(4,1)S(1)}, s32[]{:S(2)}) async-start(s8[9437184]{0:T(1024)(128)(4,1)} %bitcast.354), calls=%async_computation.12 | async-start | bytes 8388608
  1128.4 19.0 %slice-start.1 = ((s8[9437184]{0:T(1024)(128)(4,1)}), s8[4194304]{0:T(1024)(128)(4,1)S(1)}, s32[]{:S(2)}) async-start(s8[9437184]{0:T(1024)(128)(4,1)} %bitcast.354), calls=%async_computation.13 | async-start | bytes 8388608
  1128.4 19.0 %slice-start.6 = ((s8[9437184]{0:T(1024)(128)(4,1)}), s8[4194304]{0:T(1024)(128)(4,1)S(1)}, s32[]{:S(2)}) async-start(s8[9437184]{0:T(1024)(128)(4,1)} %bitcast.358), calls=%async_computation.18 | async-start | bytes 8388608
  1128.4 19.0 %slice-start.7 = ((s8[9437184]{0:T(1024)(128)(4,1)}), s8[4194304]{0:T(1024)(128)(4,1)S(1)}, s32[]{:S(2)}) async-start(s8[9437184]{0:T(1024)(128)(4,1)} %bitcast.358), calls=%async_computation.19 | async-start | bytes 8388608
  1128.4 19.0 %slice-start.9 = ((s8[4718592]{0:T(1024)(128)(4,1)}), s8[4194304]{0:T(1024)(128)(4,1)S(1)}, s32[]{:S(2)}) async-start(s8[4718592]{0:T(1024)(128)(4,1)} %bitcast.360), calls=%async_computation.21 | async-start | bytes 8388608
  1137.1 10.3 slice-start.2
  1137.1 10.3 slice-start.8
  1137.1 10.3 slice-start.10
  1154.0 3.5 copy-start.30
  1157.3 1.8 copy-start.28
  1159.0 8.7 copy-start.21
  1159.0 8.7 copy-start.22
  1159.0 8.7 copy-start.23
  1159.1 8.7 copy-start.24
  1159.1 8.7 copy-start.29
  1159.1 122.3 %copy-start.1 = (bf16[1000,768]{1,0:T(8,128)(2,1)S(1)}, bf16[1000,768]{1,0:T(8,128)(2,1)}, u32[]{:S(2)}) copy-start(bf16[1000,768]{1,0:T(8,128)(2,1)} %param.24) | copy-start | bytes 4608004
Sparse Core Ops, SparseCore 0:
  90.3 325.2 all-gather.2
  473.5 170.7 all-reduce.5
  673.8 33.9 reduce-scatter.14
  761.5 39.0 reduce-scatter.12
  803.6 324.6 all-reduce.9
  1132.1 41.2 reduce-scatter.8
  1177.4 42.4 reduce-scatter.10
  1223.6 55.6 all-reduce.7
